TPU v7x, 32 devices: a whole 2x2x4 slice. The times are simulated.
32 devices in a mesh: dp: 8 (over y, x, core), vocab: 4 (over z).
Axes of the slice: x: 2, y: 2, z: 4, core: 2. Of those that a mesh axis runs over, the one named last changes fastest.
Arguments:
- student_hidden: bfloat16 [1024, 1536], P('dp'), may hold values from -16 to 16
- head_weight: bfloat16 [1536, 16384], P('dp', 'vocab'), may hold values from -1 to 1
- teacher_logprobs: float32 [1024, 20480], P('dp', 'vocab'), may hold values from -45 to 0, as said below
- align_index: int32 [128, 2], replicated, may hold values from 0 to 159, as said below
- align_tiles: bfloat16 [128, 2, 128, 128], P('vocab'), may hold values from 0 to 6.1
- grad_scale: float32 [1024], P('dp'), may hold values from 30 to 300
Outputs:
- hidden_grad: bfloat16 [1024, 1536], P('dp', 'vocab')
- head_grad: bfloat16 [1536, 16384], P('dp', 'vocab')
Inputs may be any that keep to these rules, and one draw needn't show every extreme that they name: `teacher_logprobs`: each row's exponentials sum to 1 over the 20480 teacher entries. `align_index`: teacher block j is held by vocab index j // 40. Of the 64 entries of the student blocks held by one vocab index, at most 32 name teacher blocks held by any one vocab index, and for every vocab index some vocab index holds exactly 32 of them.
All inputs are finite; a program needn't handle non-finite values.
Results may differ from a plain program's by a relative error of at most 0.015.
Values may be sent and summed in bfloat16 or wider, within the bound.
No kernel may reach another device: no remote copies, remote signals or barrier semaphores. Data moves between devices by JAX's collectives and lax.ppermute only.
A program may use at most 128 MiB of HBM per device.

v0:
```python
import jax
import jax.numpy as jnp
from jax import lax
from jax.sharding import PartitionSpec as P

BLOCK = 128
K = 2


def pair_tables(index_rows, teacher_count, vocab_count):
    owner_of = index_rows // teacher_count
    local_block = index_rows % teacher_count
    onehot = (owner_of[..., None] == jnp.arange(vocab_count)[None, None, :]).astype(jnp.int32)
    running = jnp.cumsum(onehot, axis=1)
    slot_rank = jnp.sum(onehot * running, axis=2) - 1
    return (owner_of, local_block, slot_rank)


def gather_rows(x, axis):
    count = lax.axis_size(axis)
    copies = jnp.broadcast_to(x[None], (count,) + x.shape).reshape(
        (count * x.shape[0],) + x.shape[1:]
    )
    return lax.all_to_all(copies, axis, split_axis=0, concat_axis=0, tiled=True)


def scatter_hidden(partial):
    dp = lax.axis_size("dp")
    vocab = lax.axis_size("vocab")
    core = lax.axis_index("dp") % 2
    tokens, features = (partial.shape[0] // dp, partial.shape[1])
    parts = partial.astype(jnp.bfloat16).reshape(dp // 2, 2, tokens, features)
    kept = lax.dynamic_index_in_dim(parts, core, 1, keepdims=False)
    sent = lax.dynamic_index_in_dim(parts, 1 - core, 1, keepdims=False)
    got = lax.ppermute(sent, "dp", [(i, i ^ 1) for i in range(dp)])
    both = (kept.astype(jnp.float32) + got.astype(jnp.float32)).astype(jnp.bfloat16)
    groups = [[i for i in range(dp) if i % 2 == c] for c in range(2)]
    rows = lax.all_to_all(
        both, "dp", split_axis=0, concat_axis=0, axis_index_groups=groups, tiled=True
    )
    rows = jnp.sum(rows.astype(jnp.float32), axis=0).astype(jnp.bfloat16)
    last = rows.reshape(tokens, vocab, features // vocab).transpose(1, 0, 2)
    last = lax.all_to_all(last, "vocab", split_axis=0, concat_axis=0, tiled=True)
    return jnp.sum(last.astype(jnp.float32), axis=0).astype(jnp.bfloat16)


def body(student_hidden, head_weight, teacher_logprobs, align_index, align_tiles, grad_scale):
    vocab_count = lax.axis_size("vocab")
    dp_count = lax.axis_size("dp")
    own_index = lax.axis_index("vocab")
    dp_index = lax.axis_index("dp")
    tokens_here = student_hidden.shape[0]
    student_cols = head_weight.shape[1]
    student_count = student_cols // BLOCK
    teacher_count = teacher_logprobs.shape[1] // BLOCK
    pair_count = student_count * K
    capacity = (2 * pair_count + vocab_count - 1) // vocab_count
    all_rows = align_index.reshape(vocab_count, pair_count)
    owner_all, local_all, rank_all = pair_tables(all_rows, teacher_count, vocab_count)
    held_here = owner_all == own_index
    slot_numbers = jnp.arange(capacity)
    selected = (
        held_here[:, None, :] & (rank_all[:, None, :] == slot_numbers[None, :, None])
    ).astype(jnp.int32)
    source_block = jnp.sum(selected * local_all[:, None, :], axis=2).reshape(-1)
    own_owner = lax.dynamic_index_in_dim(owner_all, own_index, 0, keepdims=False)
    own_rank = lax.dynamic_index_in_dim(rank_all, own_index, 0, keepdims=False)
    where_from = own_owner * capacity + own_rank
    teacher_probs = (
        jnp.exp(teacher_logprobs)
        .astype(jnp.bfloat16)
        .reshape(tokens_here, teacher_count, BLOCK)
        .transpose(1, 0, 2)
    )
    outgoing = jnp.take(teacher_probs, source_block, axis=0)
    arrived = lax.all_to_all(outgoing, "vocab", split_axis=0, concat_axis=0, tiled=True)
    weight = lax.all_to_all(head_weight, "dp", split_axis=1, concat_axis=0, tiled=True)
    hidden = gather_rows(student_hidden, "dp")
    logits = jnp.dot(hidden, weight, preferred_element_type=jnp.float32)
    row_max = lax.pmax(jnp.max(logits, axis=1), ("dp", "vocab"))
    shifted = jnp.exp(logits - row_max[:, None])
    picked = jnp.take(arrived, where_from, axis=0).reshape(student_count, K, tokens_here, BLOCK)
    mapped_rows = jnp.einsum(
        "bktj,bkji->tbi", picked, align_tiles, preferred_element_type=jnp.float32
    )
    mapped_rows = mapped_rows.reshape(tokens_here, student_cols)
    mapped = lax.all_to_all(
        mapped_rows.astype(jnp.bfloat16), "dp", split_axis=1, concat_axis=0, tiled=True
    )
    own_rows = (jnp.arange(dp_count) == dp_index).astype(jnp.float32)[:, None]
    first = (own_index == 0).astype(jnp.float32)
    mass_part = (own_rows * jnp.sum(mapped_rows, axis=1)[None]).reshape(-1)
    scale_part = (own_rows * (first * grad_scale)[None]).reshape(-1)
    row_total, mass, scale = lax.psum(
        (jnp.sum(shifted, axis=1), mass_part, scale_part), ("dp", "vocab")
    )
    student_probs = shifted / row_total[:, None]
    dlogits = (
        scale[:, None] * (mass[:, None] * student_probs - mapped.astype(jnp.float32))
    ).astype(jnp.bfloat16)
    hidden_terms = lax.dot_general(
        dlogits, weight, (((1,), (1,)), ((), ())), preferred_element_type=jnp.float32
    )
    hidden_grad = scatter_hidden(hidden_terms)
    head_terms = lax.dot_general(
        hidden, dlogits, (((0,), (0,)), ((), ())), preferred_element_type=jnp.float32
    ).astype(jnp.bfloat16)
    head_grad = lax.all_to_all(head_terms, "dp", split_axis=0, concat_axis=1, tiled=True)
    return (hidden_grad, head_grad)


def solution(mesh):
    placed = (
        P("dp", None),
        P("dp", "vocab"),
        P("dp", "vocab"),
        P(),
        P("vocab", None, None, None),
        P("dp"),
    )
    return jax.shard_map(
        body,
        mesh=mesh,
        in_specs=placed,
        out_specs=(P("dp", "vocab"), P("dp", "vocab")),
        check_vma=False,
    )
```

profile of v0, /device:TPU:2, one launch (start us, length us, event | category | flops | bytes accessed | tf_op | source)
XLA Modules:
  0.0 344.2 jit_solution(2397335683305660772)
XLA Ops:
  0.6 0.0 copy-start
  0.6 2.8 copy.83
  3.5 4.4 %all-to-all-start.2 = ((bf16[192,8,512]{2,0,1:T(8,128)(2,1)}), bf16[192,8,512]{2,0,1:T(8,128)(2,1)}, u32[]{:S(2)}, u32[]{:S(2)}) async-start(bf16[192,8,512]{2,0,1:T(8,128)(2,1)} %bitcast.64), calls=%async_computation.2 | async-start | bytes 3145728 | tf_op jit(solution)/shard_map/all_to_all | solution.py:77
  7.9 0.0 copy-done.6
  7.9 0.1 copy.62
  8.1 0.1 ne.56
  8.2 0.1 copy.64
  8.3 0.1 div.26
  8.4 0.1 copy.63
  8.5 0.1 rem.44
  8.7 0.1 fusion.9
  8.8 3.2 copy.65
  12.0 3.2 exponential_convert_fusion
  15.2 0.1 reduce_window_sum.11
  15.3 0.2 select_reduce_fusion
  15.5 0.1 select_reduce_fusion.1
  15.7 0.1 reshape.197
  15.8 0.1 reshape.195
  15.9 1.8 copy.66
  17.7 3.1 gather_fusion
  20.7 4.6 %broadcast_select_fusion = bf16[128,128,128]{2,1,0:T(8,128)(2,1)} fusion(bf16[128,128,128]{2,1,0:T(8,128)(2,1)} %gather_fusion, pred[128]{0:T(512)(128)(4,1)S(1)} %compare_and_fusion.1), kind=kLoop, calls=%fused_computation.2 | loop fusion | flops 2097152 | bytes 8388736 | tf_op jit(solution)/shard_map/jit(_take)/select_n | solution.py:75
  25.3 2.1 all-to-all-done.2
  27.5 99.8 %all_to_all.72 = bf16[128,128,128]{2,1,0:T(8,128)(2,1)} all-to-all(bf16[128,128,128]{2,1,0:T(8,128)(2,1)} %broadcast_select_fusion), channel_id=1, replica_groups=mesh['dp'=8,'vocab'=4] {'vocab'}, dimensions={0} | all-to-all | bytes 8388608 | tf_op jit(solution)/shard_map/all_to_all | solution.py:76
  127.3 0.0 copy-done.5
  127.3 2.0 broadcast_in_dim.26
  129.3 4.5 %all-to-all-start.1 = ((bf16[8,128,1536]{2,1,0:T(8,128)(2,1)}), bf16[8,128,1536]{2,1,0:T(8,128)(2,1)}, u32[]{:S(2)}, u32[]{:S(2)}) async-start(bf16[8,128,1536]{2,1,0:T(8,128)(2,1)} %broadcast_in_dim.26), calls=%async_computation.1 | async-start | bytes 6291456 | tf_op jit(solution)/shard_map/all_to_all | solution.py:24
  133.8 0.5 broadcast.181
  134.3 0.7 fusion.16
  135.0 0.1 add.114
  135.1 0.0 copy-done.7
  135.2 4.3 %gather_fusion.1 = bf16[64,128,128]{2,1,0:T(8,128)(2,1)} fusion(bf16[128,128,128]{2,1,0:T(8,128)(2,1)} %all_to_all.72, s32[1024]{0:T(1024)S(1)} %pad_clamp_fusion), kind=kCustom, calls=%fused_computation.1 | custom fusion | bytes 4194560 | tf_op jit(solution)/shard_map/jit(_take)/gather | solution.py:82
  139.5 0.0 copy-done
  139.5 4.1 %bitcast_convert_fusion = (bf16[32,128,128]{1,2,0:T(8,128)(2,1)}, f32[32,128,128,1]{1,2,3,0:T(8,128)}) fusion(bf16[32,2,128,128]{3,2,1,0:T(8,128)(2,1)S(1)} %copy-done, bf16[32,2,128,128]{3,2,1,0:T(8,128)(2,1)} %bitcast.63, pred[32,2]{1,0:T(8,128)(4,1)S(1)} %compare_and_fusion), kind=kOutput, calls=%fused_computation.12 | convolution fusion | flops 270008320 | bytes 7340096 | tf_op jit(solution)/shard_map/bktj,bkji->tbi/dot_general | solution.py:83
  143.6 25.5 %all-to-all-done.1 = bf16[8,128,1536]{2,1,0:T(8,128)(2,1)} async-done(((bf16[8,128,1536]{2,1,0:T(8,128)(2,1)}), bf16[8,128,1536]{2,1,0:T(8,128)(2,1)}, u32[]{:S(2)}, u32[]{:S(2)}) %all-to-all-start.1) | async-done | bytes 3145760 | tf_op jit(solution)/shard_map/all_to_all | solution.py:24
  169.1 5.0 %all-to-all-start.3 = ((bf16[128,8,512]{0,2,1:T(8,128)(2,1)}), bf16[128,8,512]{0,2,1:T(8,128)(2,1)S(1)}, u32[]{:S(2)}, u32[]{:S(2)}) async-start(bf16[128,8,512]{0,2,1:T(8,128)(2,1)} %bitcast.14), calls=%async_computation.3 | async-start | bytes 2097152 | tf_op jit(solution)/shard_map/all_to_all | solution.py:87
  174.1 5.5 %fusion.18 = (f32[1024]{0:T(1024)S(1)}, f32[1024,512]{0,1:T(8,128)}) fusion(bf16[1024,1536]{1,0:T(8,128)(2,1)} %bitcast.10, bf16[1536,512]{1,0:T(8,128)(2,1)} %bitcast.12), kind=kOutput, calls=%fused_computation.57 | convolution fusion | flops 1611136000 | bytes 6819840 | tf_op jit(solution)/shard_map/dot_general | solution.py:79
  179.6 41.5 %pmax.7 = f32[1024]{0:T(1024)S(1)} all-reduce(f32[1024]{0:T(1024)S(1)} %get-tuple-element.15), channel_id=1, replica_groups=mesh['dp'=8,'vocab'=4] {'dp','vocab'}, use_global_device_ids=true, to_apply=%region_7.8 | all-reduce | flops 1024 | bytes 8192 | tf_op jit(solution)/shard_map/pmax | solution.py:80
  221.1 2.1 fusion.7
  223.2 0.2 copy-done.1
  223.3 0.6 bitcast_reduce_fusion
  223.9 0.1 multiply_bitcast_fusion.1
  223.9 39.5 %all-reduce = (f32[1024]{0:T(1024)S(1)}, f32[1024]{0:T(1024)S(1)}, f32[1024]{0:T(1024)S(1)}) all-reduce(f32[1024]{0:T(1024)S(1)} %fusion.7, f32[1024]{0:T(1024)S(1)} %get-tuple-element.12, f32[1024]{0:T(1024)S(1)} %get-tuple-element.11), channel_id=1, replica_groups=mesh['dp'=8,'vocab'=4] {'dp','vocab'}, use_global_device_ids=true, to_apply=%region_9.10 | all-reduce | flops 3072 | bytes 24576 | tf_op jit(solution)/shard_map/psum | solution.py:94
  263.4 0.0 all-to-all-done.3
  263.4 2.2 fusion.3
  265.6 0.0 copy-start.3
  265.6 3.6 %convolution_convert_fusion = bf16[1024,1536]{1,0:T(8,128)(2,1)S(1)} fusion(bf16[1024,512]{0,1:T(8,128)(2,1)S(1)} %fusion.3, bf16[1536,512]{1,0:T(8,128)(2,1)} %bitcast.12), kind=kOutput, calls=%fused_computation.3 | convolution fusion | flops 1612185600 | bytes 5767168 | tf_op jit(solution)/shard_map/dot_general | solution.py:101
  269.3 1.7 copy-done.2
  271.0 1.2 dynamic-slice_bitcast_fusion
  272.2 0.0 collective-permute-start
  272.2 3.7 %collective-permute-done = bf16[4,128,1536]{2,1,0:T(8,128)(2,1)} collective-permute-done((bf16[4,128,1536]{2,1,0:T(8,128)(2,1)}, bf16[4,128,1536]{2,1,0:T(8,128)(2,1)}, u32[]{:S(2)}, u32[]{:S(2)}) %collective-permute-start) | collective-permute-done | bytes 1572896 | tf_op jit(solution)/shard_map/ppermute | solution.py:35
  276.0 3.4 fusion
  279.4 4.5 %all-to-all-start.4 = ((bf16[4,128,1536]{2,1,0:T(8,128)(2,1)}), bf16[4,128,1536]{2,1,0:T(8,128)(2,1)}, u32[]{:S(2)}, u32[]{:S(2)}) async-start(bf16[4,128,1536]{2,1,0:T(8,128)(2,1)} %fusion), calls=%async_computation.4 | async-start | bytes 3145728 | tf_op jit(solution)/shard_map/all_to_all | solution.py:38
  283.9 4.9 %fusion.1 = bf16[1536,512]{0,1:T(8,128)(2,1)} fusion(bf16[1024,512]{0,1:T(8,128)(2,1)S(1)} %copy-done.4, bf16[1024,1536]{1,0:T(8,128)(2,1)} %bitcast.10), kind=kOutput, calls=%fused_computation.7 | convolution fusion | flops 1611399168 | bytes 5767168 | tf_op jit(solution)/shard_map/dot_general | solution.py:105
  288.8 2.6 copy.73
  291.4 12.1 %all-to-all-done.4 = bf16[4,128,1536]{2,1,0:T(8,128)(2,1)} async-done(((bf16[4,128,1536]{2,1,0:T(8,128)(2,1)}), bf16[4,128,1536]{2,1,0:T(8,128)(2,1)}, u32[]{:S(2)}, u32[]{:S(2)}) %all-to-all-start.4) | async-done | bytes 1572896 | tf_op jit(solution)/shard_map/all_to_all | solution.py:38
  303.5 4.8 %all-to-all-start.6 = ((bf16[8,192,512]{2,1,0:T(8,128)(2,1)}), bf16[8,192,512]{2,1,0:T(8,128)(2,1)}, u32[]{:S(2)}, u32[]{:S(2)}) async-start(bf16[8,192,512]{2,1,0:T(8,128)(2,1)} %bitcast.65), calls=%async_computation.6 | async-start | bytes 3145728 | tf_op jit(solution)/shard_map/all_to_all | solution.py:108
  308.2 1.7 reduce_sum.64
  309.9 0.2 copy.71
  310.1 0.9 copy.72
  311.0 16.8 %all-to-all-done.6 = bf16[8,192,512]{2,1,0:T(8,128)(2,1)} async-done(((bf16[8,192,512]{2,1,0:T(8,128)(2,1)}), bf16[8,192,512]{2,1,0:T(8,128)(2,1)}, u32[]{:S(2)}, u32[]{:S(2)}) %all-to-all-start.6) | async-done | bytes 1572896 | tf_op jit(solution)/shard_map/all_to_all | solution.py:108
  327.8 3.5 %all-to-all-start.5 = ((bf16[4,128,384]{2,1,0:T(8,128)(2,1)}), bf16[4,128,384]{2,1,0:T(8,128)(2,1)S(1)}, u32[]{:S(2)}, u32[]{:S(2)}) async-start(bf16[4,128,384]{2,1,0:T(8,128)(2,1)} %copy.72), calls=%async_computation.5 | async-start | bytes 786432 | tf_op jit(solution)/shard_map/all_to_all | solution.py:43
  331.3 2.7 copy.80
  334.1 9.4 %all-to-all-done.5 = bf16[4,128,384]{2,1,0:T(8,128)(2,1)S(1)} async-done(((bf16[4,128,384]{2,1,0:T(8,128)(2,1)}), bf16[4,128,384]{2,1,0:T(8,128)(2,1)S(1)}, u32[]{:S(2)}, u32[]{:S(2)}) %all-to-all-start.5) | async-done | bytes 393248 | tf_op jit(solution)/shard_map/all_to_all | solution.py:43
  343.5 0.7 reduce_sum.65
  (20 shorter events, 0.1 us)
Async XLA Ops:
  0.6 138.9 %copy-start = (bf16[32,2,128,128]{3,2,1,0:T(8,128)(2,1)S(1)}, bf16[32,2,128,128]{3,2,1,0:T(8,128)(2,1)}, u32[]{:S(2)}) copy-start(bf16[32,2,128,128]{3,2,1,0:T(8,128)(2,1)} %param.10) | copy-start | bytes 6291460
  3.5 4.4 %copy-start.6 = (s32[128,2]{0,1:T(2,128)S(1)}, s32[128,2]{0,1:T(2,128)}, u32[]{:S(2)}) copy-start(s32[128,2]{0,1:T(2,128)} %param.9) | copy-start | bytes 3076
  3.5 24.0 %all-to-all-start.2 = ((bf16[192,8,512]{2,0,1:T(8,128)(2,1)}), bf16[192,8,512]{2,0,1:T(8,128)(2,1)}, u32[]{:S(2)}, u32[]{:S(2)}) async-start(bf16[192,8,512]{2,0,1:T(8,128)(2,1)} %bitcast.64), calls=%async_computation.2 | async-start | bytes 3145728 | tf_op jit(solution)/shard_map/all_to_all | solution.py:77
  25.3 101.9 %copy-start.5 = (bf16[128,1536]{1,0:T(8,128)(2,1)S(1)}, bf16[128,1536]{1,0:T(8,128)(2,1)}, u32[]{:S(2)}) copy-start(bf16[128,1536]{1,0:T(8,128)(2,1)} %param.6) | copy-start | bytes 1179652
  129.2 5.9 %copy-start.7 = (f32[128]{0:T(128)S(1)}, f32[128]{0:T(128)}, u32[]{:S(2)}) copy-start(f32[128]{0:T(128)} %param.11) | copy-start | bytes 1540
  129.3 39.9 %all-to-all-start.1 = ((bf16[8,128,1536]{2,1,0:T(8,128)(2,1)}), bf16[8,128,1536]{2,1,0:T(8,128)(2,1)}, u32[]{:S(2)}, u32[]{:S(2)}) async-start(bf16[8,128,1536]{2,1,0:T(8,128)(2,1)} %broadcast_in_dim.26), calls=%async_computation.1 | async-start | bytes 6291456 | tf_op jit(solution)/shard_map/all_to_all | solution.py:24
  169.1 94.3 %all-to-all-start.3 = ((bf16[128,8,512]{0,2,1:T(8,128)(2,1)}), bf16[128,8,512]{0,2,1:T(8,128)(2,1)S(1)}, u32[]{:S(2)}, u32[]{:S(2)}) async-start(bf16[128,8,512]{0,2,1:T(8,128)(2,1)} %bitcast.14), calls=%async_computation.3 | async-start | bytes 2097152 | tf_op jit(solution)/shard_map/all_to_all | solution.py:87
  221.1 2.2 copy-start.1
  265.6 3.7 %copy-start.3 = (bf16[1024,512]{0,1:T(8,128)(2,1)}, bf16[1024,512]{0,1:T(8,128)(2,1)S(1)}, u32[]{:S(2)}) copy-start(bf16[1024,512]{0,1:T(8,128)(2,1)S(1)} %fusion.3) | copy-start | bytes 3145732
  269.3 1.7 copy-start.2
  272.2 3.8 %collective-permute-start = (bf16[4,128,1536]{2,1,0:T(8,128)(2,1)}, bf16[4,128,1536]{2,1,0:T(8,128)(2,1)}, u32[]{:S(2)}, u32[]{:S(2)}) collective-permute-start(bf16[4,128,1536]{2,1,0:T(8,128)(2,1)} %dynamic-slice_bitcast_fusion), channel_id=1, source_target_pairs={{0,4},{4,0},{8,12},{12,8},{16,20},{20,16},{24,28},{28,24},{1,5},{5... | collective-permute-start | bytes 4718600 | tf_op jit(solution)/shard_map/ppermute | solution.py:35
  279.4 4.5 %copy-start.4 = (bf16[1024,512]{0,1:T(8,128)(2,1)S(1)}, bf16[1024,512]{0,1:T(8,128)(2,1)}, u32[]{:S(2)}) copy-start(bf16[1024,512]{0,1:T(8,128)(2,1)} %copy-done.3) | copy-start | bytes 3145732
  279.4 24.1 %all-to-all-start.4 = ((bf16[4,128,1536]{2,1,0:T(8,128)(2,1)}), bf16[4,128,1536]{2,1,0:T(8,128)(2,1)}, u32[]{:S(2)}, u32[]{:S(2)}) async-start(bf16[4,128,1536]{2,1,0:T(8,128)(2,1)} %fusion), calls=%async_computation.4 | async-start | bytes 3145728 | tf_op jit(solution)/shard_map/all_to_all | solution.py:38
  303.5 24.4 %all-to-all-start.6 = ((bf16[8,192,512]{2,1,0:T(8,128)(2,1)}), bf16[8,192,512]{2,1,0:T(8,128)(2,1)}, u32[]{:S(2)}, u32[]{:S(2)}) async-start(bf16[8,192,512]{2,1,0:T(8,128)(2,1)} %bitcast.65), calls=%async_computation.6 | async-start | bytes 3145728 | tf_op jit(solution)/shard_map/all_to_all | solution.py:108
  327.8 15.6 %all-to-all-start.5 = ((bf16[4,128,384]{2,1,0:T(8,128)(2,1)}), bf16[4,128,384]{2,1,0:T(8,128)(2,1)S(1)}, u32[]{:S(2)}, u32[]{:S(2)}) async-start(bf16[4,128,384]{2,1,0:T(8,128)(2,1)} %copy.72), calls=%async_computation.5 | async-start | bytes 786432 | tf_op jit(solution)/shard_map/all_to_all | solution.py:43
where the time goes:
time: 345 us; the launch traced here: 344 us
  blocking collectives  181 us (52%)
  waiting for transfers between devices  69.7 us (20%)
  local copies, waits for them, and re-layouts  28.3 us (8%)
  starting transfers between devices  26.6 us (8%)
  other arithmetic  19.8 us (6%)
  matrix products  18.1 us (5%)
    all_to_all x1, blocking collectives, body(): lax.all_to_all(outgoing, 'vocab', split_axis=0, concat_axis=0, tiled=True)  99.8 us
    pmax x1, blocking collectives, body(): row_max = lax.pmax(jnp.max(logits, axis=1), ('dp', 'vocab'))  41.5 us
    psum x1, blocking collectives, body(): lax.psum((jnp.sum(shifted, axis=1), mass_part, scale_part), ('dp', 'vocab'))  39.5 us
    all_to_all x1, waiting for transfers between devices, gather_rows(): return lax.all_to_all(copies, axis, split_axis=0, concat_axis=0, tiled=True)  25.5 us
    all_to_all x1, waiting for transfers between devices, body(): lax.all_to_all(head_terms, 'dp', split_axis=0, concat_axis=1, tiled=True)  16.8 us
    all_to_all x1, waiting for transfers between devices, scatter_hidden(): lax.all_to_all(both, 'dp', split_axis=0, concat_axis=0, axis_index_groups...  12.1 us
    all_to_all x1, waiting for transfers between devices, scatter_hidden(): lax.all_to_all(last, 'vocab', split_axis=0, concat_axis=0, tiled=True)  9.4 us
  transfers between devices with their start and end apart: 7, of which 6 were waited for; matrix products, arithmetic and copies ran while one was open for 14% of the time, Pallas kernels for 0%

commit v1 on v0

--- a/solution.py
+++ b/solution.py
@@ -105,7 +105,19 @@
     head_terms = lax.dot_general(
         hidden, dlogits, (((0,), (0,)), ((), ())), preferred_element_type=jnp.float32
     ).astype(jnp.bfloat16)
-    head_grad = lax.all_to_all(head_terms, "dp", split_axis=0, concat_axis=1, tiled=True)
+    ways, here = (lax.axis_size("dp"), lax.axis_index("dp"))
+    width = head_terms.shape[0] // ways
+    dims = list(head_terms.shape)
+    dims[0] = width
+    height = dims[1]
+    dims[1] = height * ways
+    full = jnp.zeros(dims, head_terms.dtype)
+    for mask in range(ways):
+        part = lax.dynamic_slice_in_dim(head_terms, (here ^ mask) * width, width, axis=0)
+        if mask:
+            part = lax.ppermute(part, "dp", [(d, d ^ mask) for d in range(ways)])
+        full = lax.dynamic_update_slice_in_dim(full, part, (here ^ mask) * height, axis=1)
+    head_grad = full
     return (hidden_grad, head_grad)
 
 

time: 345 us -> 334 us (0.968)
  waiting for transfers between devices: 69.7 us -> 44.7 us
  local copies, waits for them, and re-layouts: 28.3 us -> 39.4 us
    all_to_all x1 -> x0, waiting for transfers between devices: 16.8 us -> none  [body(): lax.all_to_all(head_terms, 'dp', split_axis=0, concat_axis=1, tiled=True)]
    ppermute x0 -> x7, waiting for transfers between devices: none -> 13.3 us  [body(): part = lax.ppermute(part, 'dp', [(d, d ^ mask) for d in range(ways)])]
    all_to_all x1, waiting for transfers between devices: 12.1 us -> 0.01 us  [scatter_hidden(): lax.all_to_all(both, 'dp', split_axis=0, concat_axis=0, axis_index_groups...]
    all_to_all x1, waiting for transfers between devices: 9.4 us -> 0.01 us  [scatter_hidden(): lax.all_to_all(last, 'vocab', split_axis=0, concat_axis=0, tiled=True)]
    ppermute x0 -> x7, local copies, waits for them, and re-layouts: none -> 7.51 us  [body(): part = lax.ppermute(part, 'dp', [(d, d ^ mask) for d in range(ways)])]
    ppermute x0 -> x7, starting transfers between devices: none -> 6.36 us  [body(): part = lax.ppermute(part, 'dp', [(d, d ^ mask) for d in range(ways)])]
    dynamic_update_slice x0 -> x8, local copies, waits for them, and re-layouts: none -> 5.53 us  [body(): lax.dynamic_update_slice_in_dim(full, part, (here ^ mask) * height, axis=1)]
    all_to_all x1 -> x0, starting transfers between devices: 4.77 us -> none  [body(): lax.all_to_all(head_terms, 'dp', split_axis=0, concat_axis=1, tiled=True)]
  transfers between devices with their start and end apart: 7 -> 13, of which waited for: 6 -> 5; matrix products, arithmetic and copies ran while one was open for 14% -> 18% of each run, Pallas kernels for 0% -> 0%
where the time goes in v1:
time: 334 us; the launch traced here: 331 us
  blocking collectives  181 us (54%)
  waiting for transfers between devices  44.7 us (13%)
  local copies, waits for them, and re-layouts  39.4 us (12%)
  starting transfers between devices  28.8 us (9%)
  other arithmetic  19.9 us (6%)
  matrix products  16.9 us (5%)
    all_to_all x1, blocking collectives, body(): lax.all_to_all(outgoing, 'vocab', split_axis=0, concat_axis=0, tiled=True)  99.8 us
    pmax x1, blocking collectives, body(): row_max = lax.pmax(jnp.max(logits, axis=1), ('dp', 'vocab'))  41.5 us
    psum x1, blocking collectives, body(): lax.psum((jnp.sum(shifted, axis=1), mass_part, scale_part), ('dp', 'vocab'))  39.5 us
    all_to_all x1, waiting for transfers between devices, gather_rows(): return lax.all_to_all(copies, axis, split_axis=0, concat_axis=0, tiled=True)  25.5 us
    ppermute x7, waiting for transfers between devices, body(): part = lax.ppermute(part, 'dp', [(d, d ^ mask) for d in range(ways)])  13.3 us
    ppermute x7, local copies, waits for them, and re-layouts, body(): part = lax.ppermute(part, 'dp', [(d, d ^ mask) for d in range(ways)])  7.51 us
  transfers between devices with their start and end apart: 13, of which 5 were waited for; matrix products, arithmetic and copies ran while one was open for 18% of the time, Pallas kernels for 0%

profile of v1, /device:TPU:2, one launch (start us, length us, event | category | flops | bytes accessed | tf_op | source)
XLA Modules:
  0.0 331.5 jit_solution(17894899028369791902)
XLA Ops:
  0.6 2.8 copy.126
  3.5 4.4 %all-to-all-start.2 = ((bf16[192,8,512]{2,0,1:T(8,128)(2,1)}), bf16[192,8,512]{2,0,1:T(8,128)(2,1)}, u32[]{:S(2)}, u32[]{:S(2)}) async-start(bf16[192,8,512]{2,0,1:T(8,128)(2,1)} %bitcast.74), calls=%async_computation.2 | async-start | bytes 3145728 | tf_op jit(solution)/shard_map/all_to_all | solution.py:77
  8.4 0.1 copy.100
  8.8 3.2 copy.103
  12.0 3.2 exponential_convert_fusion
  15.2 0.1 reduce_window_sum.11
  15.3 0.2 select_reduce_fusion
  15.6 0.1 select_reduce_fusion.1
  15.9 1.8 copy.104
  17.7 3.1 gather_fusion
  20.7 4.6 %broadcast_select_fusion = bf16[128,128,128]{2,1,0:T(8,128)(2,1)} fusion(bf16[128,128,128]{2,1,0:T(8,128)(2,1)} %gather_fusion, pred[128]{0:T(512)(128)(4,1)S(1)} %compare_and_fusion.1), kind=kLoop, calls=%fused_computation.2 | loop fusion | flops 2097152 | bytes 8388736 | tf_op jit(solution)/shard_map/jit(_take)/select_n | solution.py:75
  25.4 2.1 all-to-all-done.2
  27.5 99.8 %all_to_all.53 = bf16[128,128,128]{2,1,0:T(8,128)(2,1)} all-to-all(bf16[128,128,128]{2,1,0:T(8,128)(2,1)} %broadcast_select_fusion), channel_id=1, replica_groups=mesh['dp'=8,'vocab'=4] {'vocab'}, dimensions={0} | all-to-all | bytes 8388608 | tf_op jit(solution)/shard_map/all_to_all | solution.py:76
  127.3 2.0 broadcast_in_dim.28
  129.2 4.5 %all-to-all-start.1 = ((bf16[8,128,1536]{2,1,0:T(8,128)(2,1)}), bf16[8,128,1536]{2,1,0:T(8,128)(2,1)}, u32[]{:S(2)}, u32[]{:S(2)}) async-start(bf16[8,128,1536]{2,1,0:T(8,128)(2,1)} %broadcast_in_dim.28), calls=%async_computation.1 | async-start | bytes 6291456 | tf_op jit(solution)/shard_map/all_to_all | solution.py:24
  133.8 0.5 broadcast.181
  134.3 0.7 fusion.15
  135.2 4.3 %gather_fusion.1 = bf16[64,128,128]{2,1,0:T(8,128)(2,1)} fusion(bf16[128,128,128]{2,1,0:T(8,128)(2,1)} %all_to_all.53, s32[1024]{0:T(1024)S(1)} %pad_clamp_fusion), kind=kCustom, calls=%fused_computation.1 | custom fusion | bytes 4194560 | tf_op jit(solution)/shard_map/jit(_take)/gather | solution.py:82
  139.5 4.1 %bitcast_convert_fusion = (bf16[32,128,128]{1,2,0:T(8,128)(2,1)}, f32[32,128,128,1]{1,2,3,0:T(8,128)}) fusion(bf16[32,2,128,128]{3,2,1,0:T(8,128)(2,1)S(1)} %copy-done, bf16[32,2,128,128]{3,2,1,0:T(8,128)(2,1)} %bitcast.73, pred[32,2]{1,0:T(8,128)(4,1)S(1)} %compare_and_fusion), kind=kOutput, calls=%fused_computation.11 | convolution fusion | flops 270008320 | bytes 7340096 | tf_op jit(solution)/shard_map/bktj,bkji->tbi/dot_general | solution.py:83
  143.6 25.5 %all-to-all-done.1 = bf16[8,128,1536]{2,1,0:T(8,128)(2,1)} async-done(((bf16[8,128,1536]{2,1,0:T(8,128)(2,1)}), bf16[8,128,1536]{2,1,0:T(8,128)(2,1)}, u32[]{:S(2)}, u32[]{:S(2)}) %all-to-all-start.1) | async-done | bytes 3145760 | tf_op jit(solution)/shard_map/all_to_all | solution.py:24
  169.1 5.0 %all-to-all-start.3 = ((bf16[128,8,512]{0,2,1:T(8,128)(2,1)}), bf16[128,8,512]{0,2,1:T(8,128)(2,1)S(1)}, u32[]{:S(2)}, u32[]{:S(2)}) async-start(bf16[128,8,512]{0,2,1:T(8,128)(2,1)} %bitcast.14), calls=%async_computation.3 | async-start | bytes 2097152 | tf_op jit(solution)/shard_map/all_to_all | solution.py:87
  174.1 5.5 %fusion.17 = (f32[1024]{0:T(1024)S(1)}, f32[1024,512]{0,1:T(8,128)}) fusion(bf16[1024,1536]{1,0:T(8,128)(2,1)} %bitcast.10, bf16[1536,512]{1,0:T(8,128)(2,1)} %bitcast.12), kind=kOutput, calls=%fused_computation.72 | convolution fusion | flops 1611136000 | bytes 6819840 | tf_op jit(solution)/shard_map/dot_general | solution.py:79
  179.6 41.5 %pmax.7 = f32[1024]{0:T(1024)S(1)} all-reduce(f32[1024]{0:T(1024)S(1)} %get-tuple-element.23), channel_id=1, replica_groups=mesh['dp'=8,'vocab'=4] {'dp','vocab'}, use_global_device_ids=true, to_apply=%region_7.8 | all-reduce | flops 1024 | bytes 8192 | tf_op jit(solution)/shard_map/pmax | solution.py:80
  221.1 2.1 fusion.6
  223.1 0.2 copy-done.1
  223.3 0.6 bitcast_reduce_fusion
  223.9 39.5 %all-reduce = (f32[1024]{0:T(1024)S(1)}, f32[1024]{0:T(1024)S(1)}, f32[1024]{0:T(1024)S(1)}) all-reduce(f32[1024]{0:T(1024)S(1)} %fusion.6, f32[1024]{0:T(1024)S(1)} %get-tuple-element.20, f32[1024]{0:T(1024)S(1)} %get-tuple-element.19), channel_id=1, replica_groups=mesh['dp'=8,'vocab'=4] {'dp','vocab'}, use_global_device_ids=true, to_apply=%region_9.10 | all-reduce | flops 3072 | bytes 24576 | tf_op jit(solution)/shard_map/psum | solution.py:94
  263.4 2.2 fusion.2
  265.6 3.6 %convolution_convert_fusion = bf16[1024,1536]{1,0:T(8,128)(2,1)S(1)} fusion(bf16[1024,512]{0,1:T(8,128)(2,1)S(1)} %fusion.2, bf16[1536,512]{1,0:T(8,128)(2,1)} %bitcast.12), kind=kOutput, calls=%fused_computation.3 | convolution fusion | flops 1612185600 | bytes 5767168 | tf_op jit(solution)/shard_map/dot_general | solution.py:101
  269.3 1.6 copy-done.2
  270.9 1.2 dynamic-slice_bitcast_fusion
  272.2 3.7 %collective-permute-done = bf16[4,128,1536]{2,1,0:T(8,128)(2,1)} collective-permute-done((bf16[4,128,1536]{2,1,0:T(8,128)(2,1)}, bf16[4,128,1536]{2,1,0:T(8,128)(2,1)}, u32[]{:S(2)}, u32[]{:S(2)}) %collective-permute-start) | collective-permute-done | bytes 1572896 | tf_op jit(solution)/shard_map/ppermute | solution.py:35
  275.9 3.5 %fusion = bf16[4,128,1536]{2,1,0:T(8,128)(2,1)} fusion(bf16[4,128,1536]{2,1,0:T(8,128)(2,1)} %collective-permute-done, bf16[4,2,128,1536]{3,2,1,0:T(8,128)(2,1)} %bitcast.77, s32[]{:T(128)S(6)} %select_n.142), kind=kLoop, calls=%fused_computation.5 | loop fusion | flops 3145728 | bytes 4718596 | tf_op jit(solution)/shard_map/convert_element_type | solution.py:36
  279.4 4.5 %all-to-all-start.4 = ((bf16[4,128,1536]{2,1,0:T(8,128)(2,1)}), bf16[4,128,1536]{2,1,0:T(8,128)(2,1)}, u32[]{:S(2)}, u32[]{:S(2)}) async-start(bf16[4,128,1536]{2,1,0:T(8,128)(2,1)} %fusion), calls=%async_computation.4 | async-start | bytes 3145728 | tf_op jit(solution)/shard_map/all_to_all | solution.py:38
  284.0 3.7 %convolution_convert_fusion.1 = bf16[512,1536]{1,0:T(8,128)(2,1)S(1)} fusion(bf16[1024,512]{0,1:T(8,128)(2,1)S(1)} %copy-done.4, bf16[1024,1536]{1,0:T(8,128)(2,1)} %bitcast.10), kind=kOutput, calls=%fused_computation.6 | convolution fusion | flops 1611399168 | bytes 5767168 | tf_op jit(solution)/shard_map/dot_general | solution.py:105
  287.6 2.0 dynamic-slice_bitcast_fusion.1
  289.9 1.8 collective-permute-start.3
  291.7 1.1 collective-permute-start.4
  292.9 0.6 collective-permute-start.5
  293.5 1.3 broadcast_in_dim.29
  294.8 0.7 constant_dynamic-update-slice_fusion.6
  295.5 1.5 collective-permute-start.6
  297.0 1.1 copy.112
  298.1 10.0 %collective-permute-done.2 = bf16[192,512]{0,1:T(8,128)(2,1)} collective-permute-done((bf16[192,512]{0,1:T(8,128)(2,1)S(1)}, bf16[192,512]{0,1:T(8,128)(2,1)}, u32[]{:S(2)}, u32[]{:S(2)}) %collective-permute-start.2) | collective-permute-done | bytes 196640 | tf_op jit(solution)/shard_map/ppermute | solution.py:118
  308.0 1.2 collective-permute-start.7
  309.2 1.1 copy.113
  310.3 0.7 constant_dynamic-update-slice_fusion.5
  311.0 1.7 reduce_sum.64
  312.6 0.2 copy.109
  312.9 0.9 copy.110
  313.8 4.1 %all-to-all-start.5 = ((bf16[4,128,384]{2,1,0:T(8,128)(2,1)}), bf16[4,128,384]{2,1,0:T(8,128)(2,1)S(1)}, u32[]{:S(2)}, u32[]{:S(2)}) async-start(bf16[4,128,384]{2,1,0:T(8,128)(2,1)} %copy.110), calls=%async_computation.5 | async-start | bytes 786432 | tf_op jit(solution)/shard_map/all_to_all | solution.py:43
  317.9 0.7 constant_dynamic-update-slice_fusion.4
  318.6 1.1 copy.114
  319.7 1.1 copy.115
  320.8 3.3 collective-permute-done.5
  324.1 1.1 copy.116
  325.2 1.1 copy.117
  326.2 1.1 copy.118
  327.3 0.7 constant_dynamic-update-slice_fusion.3
  328.0 0.7 constant_dynamic-update-slice_fusion.2
  328.7 0.7 constant_dynamic-update-slice_fusion.1
  329.4 0.7 constant_dynamic-update-slice_fusion
  330.1 0.7 constant_dynamic-update-slice_fusion.7
  330.8 0.7 reduce_sum.65
  (48 shorter events, 1.4 us)
Async XLA Ops:
  0.6 138.8 %copy-start = (bf16[32,2,128,128]{3,2,1,0:T(8,128)(2,1)S(1)}, bf16[32,2,128,128]{3,2,1,0:T(8,128)(2,1)}, u32[]{:S(2)}) copy-start(bf16[32,2,128,128]{3,2,1,0:T(8,128)(2,1)} %param.10) | copy-start | bytes 6291460
  3.5 4.4 %copy-start.6 = (s32[128,2]{0,1:T(2,128)S(1)}, s32[128,2]{0,1:T(2,128)}, u32[]{:S(2)}) copy-start(s32[128,2]{0,1:T(2,128)} %param.9) | copy-start | bytes 3076
  3.5 24.0 %all-to-all-start.2 = ((bf16[192,8,512]{2,0,1:T(8,128)(2,1)}), bf16[192,8,512]{2,0,1:T(8,128)(2,1)}, u32[]{:S(2)}, u32[]{:S(2)}) async-start(bf16[192,8,512]{2,0,1:T(8,128)(2,1)} %bitcast.74), calls=%async_computation.2 | async-start | bytes 3145728 | tf_op jit(solution)/shard_map/all_to_all | solution.py:77
  25.4 101.9 %copy-start.5 = (bf16[128,1536]{1,0:T(8,128)(2,1)S(1)}, bf16[128,1536]{1,0:T(8,128)(2,1)}, u32[]{:S(2)}) copy-start(bf16[128,1536]{1,0:T(8,128)(2,1)} %param.6) | copy-start | bytes 1179652
  129.2 5.9 %copy-start.7 = (f32[128]{0:T(128)S(1)}, f32[128]{0:T(128)}, u32[]{:S(2)}) copy-start(f32[128]{0:T(128)} %param.11) | copy-start | bytes 1540
  129.2 39.9 %all-to-all-start.1 = ((bf16[8,128,1536]{2,1,0:T(8,128)(2,1)}), bf16[8,128,1536]{2,1,0:T(8,128)(2,1)}, u32[]{:S(2)}, u32[]{:S(2)}) async-start(bf16[8,128,1536]{2,1,0:T(8,128)(2,1)} %broadcast_in_dim.28), calls=%async_computation.1 | async-start | bytes 6291456 | tf_op jit(solution)/shard_map/all_to_all | solution.py:24
  169.1 94.3 %all-to-all-start.3 = ((bf16[128,8,512]{0,2,1:T(8,128)(2,1)}), bf16[128,8,512]{0,2,1:T(8,128)(2,1)S(1)}, u32[]{:S(2)}, u32[]{:S(2)}) async-start(bf16[128,8,512]{0,2,1:T(8,128)(2,1)} %bitcast.14), calls=%async_computation.3 | async-start | bytes 2097152 | tf_op jit(solution)/shard_map/all_to_all | solution.py:87
  221.1 2.2 copy-start.1
  265.6 3.7 %copy-start.3 = (bf16[1024,512]{0,1:T(8,128)(2,1)}, bf16[1024,512]{0,1:T(8,128)(2,1)S(1)}, u32[]{:S(2)}) copy-start(bf16[1024,512]{0,1:T(8,128)(2,1)S(1)} %fusion.2) | copy-start | bytes 3145732
  269.3 1.7 copy-start.2
  272.2 3.8 %collective-permute-start = (bf16[4,128,1536]{2,1,0:T(8,128)(2,1)}, bf16[4,128,1536]{2,1,0:T(8,128)(2,1)}, u32[]{:S(2)}, u32[]{:S(2)}) collective-permute-start(bf16[4,128,1536]{2,1,0:T(8,128)(2,1)} %dynamic-slice_bitcast_fusion), channel_id=1, source_target_pairs={{0,4},{4,0},{8,12},{12,8},{16,20},{20,16},{24,28},{28,24},{1,5},{5... | collective-permute-start | bytes 4718600 | tf_op jit(solution)/shard_map/ppermute | solution.py:35
  279.4 4.5 %copy-start.4 = (bf16[1024,512]{0,1:T(8,128)(2,1)S(1)}, bf16[1024,512]{0,1:T(8,128)(2,1)}, u32[]{:S(2)}) copy-start(bf16[1024,512]{0,1:T(8,128)(2,1)} %copy-done.3) | copy-start | bytes 3145732
  279.4 31.5 %all-to-all-start.4 = ((bf16[4,128,1536]{2,1,0:T(8,128)(2,1)}), bf16[4,128,1536]{2,1,0:T(8,128)(2,1)}, u32[]{:S(2)}, u32[]{:S(2)}) async-start(bf16[4,128,1536]{2,1,0:T(8,128)(2,1)} %fusion), calls=%async_computation.4 | async-start | bytes 3145728 | tf_op jit(solution)/shard_map/all_to_all | solution.py:38
  289.7 5.8 %collective-permute-start.1 = (bf16[192,512]{0,1:T(8,128)(2,1)S(1)}, bf16[192,512]{0,1:T(8,128)(2,1)}, u32[]{:S(2)}, u32[]{:S(2)}) collective-permute-start(bf16[192,512]{0,1:T(8,128)(2,1)S(1)} %get-tuple-element.15), channel_id=1, source_target_pairs={{0,4},{4,0},{8,12},{12,8},{16,20},{20,16},{24,28},{28,24},{1,5},{5... | collective-permute-start | bytes 589832 | tf_op jit(solution)/shard_map/ppermute | solution.py:118
  289.8 18.2 %collective-permute-start.2 = (bf16[192,512]{0,1:T(8,128)(2,1)S(1)}, bf16[192,512]{0,1:T(8,128)(2,1)}, u32[]{:S(2)}, u32[]{:S(2)}) collective-permute-start(bf16[192,512]{0,1:T(8,128)(2,1)S(1)} %get-tuple-element.14), channel_id=1, source_target_pairs={{0,8},{4,12},{8,0},{12,4},{16,24},{20,28},{24,16},{28,20},{1,9},{5... | collective-permute-start | bytes 589832 | tf_op jit(solution)/shard_map/ppermute | solution.py:118
  289.9 28.7 %collective-permute-start.3 = (bf16[192,512]{0,1:T(8,128)(2,1)}, bf16[192,512]{0,1:T(8,128)(2,1)}, u32[]{:S(2)}, u32[]{:S(2)}) collective-permute-start(bf16[192,512]{0,1:T(8,128)(2,1)} %get-tuple-element.13), channel_id=1, source_target_pairs={{0,12},{4,8},{8,4},{12,0},{16,28},{20,24},{24,20},{28,16},{1,13},{... | collective-permute-start | bytes 589832 | tf_op jit(solution)/shard_map/ppermute | solution.py:118
  291.7 27.9 %collective-permute-start.4 = (bf16[192,512]{0,1:T(8,128)(2,1)}, bf16[192,512]{0,1:T(8,128)(2,1)}, u32[]{:S(2)}, u32[]{:S(2)}) collective-permute-start(bf16[192,512]{0,1:T(8,128)(2,1)} %get-tuple-element.12), channel_id=1, source_target_pairs={{0,16},{4,20},{8,24},{12,28},{16,0},{20,4},{24,8},{28,12},{1,17},{... | collective-permute-start | bytes 589832 | tf_op jit(solution)/shard_map/ppermute | solution.py:118
  292.9 31.2 %collective-permute-start.5 = (bf16[192,512]{0,1:T(8,128)(2,1)}, bf16[192,512]{0,1:T(8,128)(2,1)}, u32[]{:S(2)}, u32[]{:S(2)}) collective-permute-start(bf16[192,512]{0,1:T(8,128)(2,1)} %get-tuple-element.11), channel_id=1, source_target_pairs={{0,20},{4,16},{8,28},{12,24},{16,4},{20,0},{24,12},{28,8},{1,21},{... | collective-permute-start | bytes 589832 | tf_op jit(solution)/shard_map/ppermute | solution.py:118
  295.5 29.7 %collective-permute-start.6 = (bf16[192,512]{0,1:T(8,128)(2,1)}, bf16[192,512]{0,1:T(8,128)(2,1)}, u32[]{:S(2)}, u32[]{:S(2)}) collective-permute-start(bf16[192,512]{0,1:T(8,128)(2,1)} %get-tuple-element.10), channel_id=1, source_target_pairs={{0,24},{4,28},{8,16},{12,20},{16,8},{20,12},{24,0},{28,4},{1,25},{... | collective-permute-start | bytes 589832 | tf_op jit(solution)/shard_map/ppermute | solution.py:118
  308.0 18.2 %collective-permute-start.7 = (bf16[192,512]{0,1:T(8,128)(2,1)S(1)}, bf16[192,512]{0,1:T(8,128)(2,1)}, u32[]{:S(2)}, u32[]{:S(2)}) collective-permute-start(bf16[192,512]{0,1:T(8,128)(2,1)S(1)} %get-tuple-element.9), channel_id=1, source_target_pairs={{0,28},{4,24},{8,20},{12,16},{16,12},{20,8},{24,4},{28,0},{1,29},{... | collective-permute-start | bytes 589832 | tf_op jit(solution)/shard_map/ppermute | solution.py:118
  313.8 17.0 %all-to-all-start.5 = ((bf16[4,128,384]{2,1,0:T(8,128)(2,1)}), bf16[4,128,384]{2,1,0:T(8,128)(2,1)S(1)}, u32[]{:S(2)}, u32[]{:S(2)}) async-start(bf16[4,128,384]{2,1,0:T(8,128)(2,1)} %copy.110), calls=%async_computation.5 | async-start | bytes 786432 | tf_op jit(solution)/shard_map/all_to_all | solution.py:43
